TPU v7x, 32 devices: a whole 2x2x4 slice. The times are simulated.
32 devices in a mesh: parts: 2 (over x), slab: 8 (over z, y), freq: 2 (over core).
Axes of the slice: x: 2, y: 2, z: 4, core: 2. Of those that a mesh axis runs over, the one named last changes fastest.
Arguments:
- reflectivity: float32 [65536], P(('parts', 'slab')), parts along dimension 0, may hold values from -6 to 6
- source_green: bfloat16 [4, 65536, 2, 256], P('freq', ('parts', 'slab')), parts along dimension 1, may hold values from -6 to 6
- receiver_green: bfloat16 [4, 65536, 2, 256], P('freq', ('parts', 'slab')), parts along dimension 1, may hold values from -0.03125 to 0.03125
- observed: float32 [4, 32, 2, 128, 128], P('freq', ('parts', 'slab')), parts along dimension 1, may hold values from -6 to 6
- source_table: int32 [16, 2], P(('parts', 'slab')), parts along dimension 0, may hold values from 0 to 3, as said below
- receiver_table: int32 [16, 2], P(('parts', 'slab')), parts along dimension 0, may hold values from 0 to 3, as said below
Outputs:
- gradient: float32 [65536], P(('parts', 'slab', 'freq')), parts along dimension 0
- residual: float32 [4, 32, 2, 128, 128], P('freq', ('parts', 'slab')), parts along dimension 1
There are 2 independent parts, one for each index of `parts`. A program takes and returns all parts, laid end to end along the dimension named above; each array names one. Nothing has to cross between parts.
Inputs may be any that keep to these rules, and one draw needn't show every extreme that they name: `source_table`: each row lists 2 different source blocks. `receiver_table`: each row lists 2 different receiver blocks.
All inputs are finite; a program needn't handle non-finite values.
Results may differ from a plain program's by a relative error of at most 0.0016.
Values may be sent and summed in bfloat16 or wider, within the bound.
A program may use at most 128 MiB of HBM per device.

v0:
```python
import jax
import jax.numpy as jnp
from jax import lax
from jax.sharding import PartitionSpec as P

RB = 4


def on_device(reflectivity, source_green, receiver_green, observed, source_table, receiver_table):
    freq_local = source_green.shape[0]
    point_local = source_green.shape[1]
    block_width = observed.shape[3]
    src_count = source_table.shape[1]
    rec_count = receiver_table.shape[1]
    panels_local = observed.shape[1]
    slab_count = lax.axis_size("slab")
    panel_total = panels_local * slab_count
    pair_count = src_count * rec_count
    panel_ids = (source_table[0][:, None] * RB + receiver_table[0][None, :]).reshape(-1)
    onehot = (panel_ids[:, None] == jnp.arange(panel_total, dtype=jnp.int32)[None, :]).astype(
        jnp.float32
    )
    scaled = (source_green * reflectivity[None, :, None, None]).astype(jnp.bfloat16)
    products = jnp.einsum(
        "fmas,fmbr->fasbr", scaled, receiver_green, preferred_element_type=jnp.float32
    )
    real_part = products[:, 0, :, 0, :] - products[:, 1, :, 1, :]
    imag_part = products[:, 0, :, 1, :] + products[:, 1, :, 0, :]
    stacked = jnp.stack([real_part, imag_part], axis=1)
    stacked = stacked.reshape(freq_local, 2, src_count, block_width, rec_count, block_width)
    partial_value = stacked.transpose(0, 2, 4, 1, 3, 5).reshape(
        freq_local, pair_count, 2, block_width, block_width
    )
    spread = jnp.einsum("kp,fkcxy->fpcxy", onehot, partial_value, precision=lax.Precision.HIGHEST)
    own_pred = lax.psum_scatter(spread, "slab", scatter_dimension=1, tiled=True)
    residual = own_pred - observed
    everyone = lax.all_gather(residual.astype(jnp.bfloat16), "slab", axis=1, tiled=True)
    local_res = jnp.einsum(
        "kp,fpcxy->fkcxy", onehot.astype(jnp.bfloat16), everyone, preferred_element_type=jnp.float32
    ).astype(jnp.bfloat16)
    local_res = local_res.reshape(
        freq_local, src_count, rec_count, 2, block_width, block_width
    ).transpose(0, 1, 4, 3, 2, 5)
    local_res = local_res.reshape(freq_local, src_count * block_width, 2, rec_count * block_width)
    gradient = jnp.zeros((point_local,), jnp.float32)
    for freq_step in range(freq_local):
        adjoint = jnp.einsum(
            "onu,uth->onth",
            source_green[freq_step],
            local_res[freq_step],
            preferred_element_type=jnp.float32,
        )
        adj_real = adjoint[:, 0, 0] + adjoint[:, 1, 1]
        adj_imag = adjoint[:, 0, 1] - adjoint[:, 1, 0]
        terms = (
            receiver_green[freq_step, :, 0] * adj_real + receiver_green[freq_step, :, 1] * adj_imag
        )
        gradient = gradient + jnp.sum(terms, axis=1)
    return (lax.psum_scatter(gradient, "freq", scatter_dimension=0, tiled=True), residual)


def solution(mesh):
    return jax.shard_map(
        on_device,
        mesh=mesh,
        in_specs=(
            P(("parts", "slab")),
            P("freq", ("parts", "slab"), None, None),
            P("freq", ("parts", "slab"), None, None),
            P("freq", ("parts", "slab"), None, None, None),
            P(("parts", "slab"), None),
            P(("parts", "slab"), None),
        ),
        out_specs=(P(("parts", "slab", "freq")), P("freq", ("parts", "slab"), None, None, None)),
        check_vma=False,
    )
```

profile of v0, /device:TPU:0, one launch (start us, length us, event | category | flops | bytes accessed | tf_op | source)
XLA Modules:
  0.0 243.8 jit_solution(1133530731579320437)
XLA Ops:
  7.2 0.0 reduce-scatter.2.cloned.1.call-start
  7.2 13.2 %fusion.3 = bf16[2,4096,2,256,1]{3,2,1,0,4:T(2,128)(2,1)} fusion(f32[4096]{0:T(1024)} %param.6, bf16[2,4096,2,256]{3,2,1,0:T(2,128)(2,1)} %param.7), kind=kLoop, calls=%fused_computation.6 | loop fusion | flops 12582912 | bytes 16793600 | tf_op jit(solution)/shard_map/convert_element_type | solution.py:23
  20.4 9.5 %fusion = f32[2,2,256,2,256]{4,2,3,1,0:T(8,128)S(1)} fusion(bf16[2,4096,2,256,1]{3,2,1,0,4:T(2,128)(2,1)} %bitcast.126, bf16[2,4096,2,256,1]{3,2,1,0,4:T(2,128)(2,1)} %fusion.3), kind=kOutput, calls=%fused_computation.3 | convolution fusion | flops 4294967296 | bytes 18874368 | tf_op jit(solution)/shard_map/fmas,fmbr->fasbr/dot_general | solution.py:24
  29.8 0.0 copy-start.6
  29.8 0.0 copy-start.5
  29.9 0.1 slice_subtract_fusion.2
  30.0 0.3 add.62
  30.3 0.3 sub.30
  30.6 0.5 maximum_bitcast_fusion
  31.1 0.4 copy.28
  31.5 0.0 copy-done.6
  31.5 0.0 copy-done.5
  31.5 0.1 broadcast_add_fusion
  31.6 0.1 add.67
  31.7 1.9 convolution_bitcast_fusion.2
  33.6 3.2 %copy.29 = f32[2,16,2,128,128]{4,3,2,0,1:T(8,128)} copy(f32[2,16,2,128,128]{4,1,3,2,0:T(8,128)S(1)} %convolution_bitcast_fusion.2) | data formatting | bytes 8388608 | tf_op jit(solution)/shard_map/kp,fkcxy->fpcxy/transpose | solution.py:34
  36.8 0.0 copy-start.4
  36.8 0.0 reduce-scatter.2.cloned.1.call-update
  36.8 0.2 all-gather.2.cloned.1.call-start
  37.1 91.0 %reduce-scatter.2.cloned.1.call-done = f32[2,2,2,128,128]{4,3,2,0,1:T(8,128)} async-done(((f32[2,16,2,128,128]{4,3,2,0,1:T(8,128)}), f32[2,2,2,128,128]{4,3,2,0,1:T(8,128)}) %reduce-scatter.2.cloned.1.call-update) | async-done | bytes 524304 | tf_op jit(solution)/shard_map/reduce_scatter | solution.py:35
  128.0 0.0 copy-done.4
  128.0 1.8 fusion.31
  129.9 0.0 all-gather.2.cloned.1.call-update
  129.9 19.4 %fusion.32 = (bf16[1,4096,1,256]{3,2,1,0:T(2,128)(2,1)}, bf16[1,4096,1,256]{3,2,1,0:T(2,128)(2,1)}, bf16[1,4096,1,256]{3,2,1,0:T(2,128)(2,1)}, bf16[1,4096,1,256]{3,2,1,0:T(2,128)(2,1)}) fusion(bf16[2,4096,2,256]{3,2,1,0:T(2,128)(2,1)} %param.8), kind=kLoop, calls=%fused_computation.48 | loop fusion | bytes 16777216 | tf_op jit(solution)/shard_map/slice | solution.py:56
  149.3 8.6 %copy.63 = bf16[1,4096,1,256]{1,3,2,0:T(8,128)(2,1)S(1)} copy(bf16[1,4096,1,256]{3,2,1,0:T(2,128)(2,1)} %get-tuple-element.11) | data formatting | bytes 4194304
  157.9 9.7 %copy.59 = bf16[1,4096,1,256]{1,3,2,0:T(8,128)(2,1)} copy(bf16[1,4096,1,256]{3,2,1,0:T(2,128)(2,1)} %get-tuple-element.8) | data formatting | bytes 4194304
  167.7 9.8 %copy.58 = bf16[1,4096,1,256]{1,3,2,0:T(8,128)(2,1)} copy(bf16[1,4096,1,256]{3,2,1,0:T(2,128)(2,1)} %get-tuple-element.9) | data formatting | bytes 4194304
  177.4 9.7 %copy.54 = bf16[1,4096,1,256]{1,3,2,0:T(8,128)(2,1)} copy(bf16[1,4096,1,256]{3,2,1,0:T(2,128)(2,1)} %get-tuple-element.10) | data formatting | bytes 4194304
  187.2 0.0 copy-done.7
  187.2 0.6 dynamic-slice
  188.4 8.4 %fusion.33 = (bf16[1,4096,2,256]{3,2,1,0:T(2,128)(2,1)}, bf16[1,4096,2,256]{3,2,1,0:T(2,128)(2,1)}) fusion(bf16[2,4096,2,256]{3,2,1,0:T(2,128)(2,1)} %param.7), kind=kLoop, calls=%fused_computation.49 | loop fusion | bytes 16777216 | tf_op jit(solution)/shard_map/slice | solution.py:49
  196.9 0.8 copy.43
  197.7 2.9 %fusion.20 = bf16[2,2,128,128,4]{3,4,2,1,0:T(4,128)(2,1)S(1)} fusion(bf16[2,16,2,128,128]{4,3,2,0,1:T(8,128)(2,1)} %all-gather.2.cloned.1.call-done, s32[4]{0:T(128)S(1)} %add.67), kind=kOutput, calls=%fused_computation.32 | convolution fusion | flops 8650944 | bytes 2621456 | tf_op jit(solution)/shard_map/kp,fpcxy->fkcxy/dot_general | solution.py:38
  200.6 0.4 fusion.34
  201.0 0.3 copy.38
  201.3 0.2 reshape.106
  201.5 0.3 copy.32
  201.8 0.2 reshape.104
  202.0 0.0 copy-start
  202.0 10.5 %convolution_bitcast_fusion = f32[4096,2,2,256]{0,3,1,2:T(8,128)} fusion(bf16[1,4096,2,256]{3,2,1,0:T(2,128)(2,1)} %get-tuple-element.12, bf16[256,2,256,1]{0,2,1,3:T(8,128)(2,1)S(1)} %reshape.106), kind=kOutput, calls=%fused_computation.1 | convolution fusion | flops 2147483648 | bytes 21233664 | tf_op jit(solution)/shard_map/onu,uth->onth/dot_general | solution.py:47
  212.4 0.0 copy-done
  212.5 8.1 %convolution_bitcast_fusion.1 = f32[4096,2,2,256]{0,3,1,2:T(8,128)} fusion(bf16[1,4096,2,256]{3,2,1,0:T(2,128)(2,1)S(1)} %copy-done, bf16[256,2,256,1]{0,2,1,3:T(8,128)(2,1)S(1)} %reshape.104), kind=kOutput, calls=%fused_computation.2 | convolution fusion | flops 2147483648 | bytes 21233664 | tf_op jit(solution)/shard_map/onu,uth->onth/dot_general | solution.py:47
  220.6 0.0 copy-done.1
  220.6 0.0 copy-done.2
  220.6 0.0 copy-done.3
  220.6 12.4 %fusion.7 = (f32[4096]{0:T(1024)S(1)}, f32[4096]{0:T(1024)S(1)}) fusion(f32[4096,2,2,256]{0,3,1,2:T(8,128)} %convolution_bitcast_fusion, bf16[1,4096,1,256]{1,3,2,0:T(8,128)(2,1)S(1)} %copy.63, bf16[1,4096,1,256]{1,3,2,0:T(8,128)(2,1)S(1)} %copy-done.1, f32[4096,2,2,256]{0,3,1,2:T(8,128)} %convolution_bitcast_fusion.1, ...), kind=kLoop, calls=%fused_computation.11 | loop fusion | flops 16769024 | bytes 41975808 | tf_op jit(solution)/shard_map/reduce_sum | solution.py:58
  233.0 3.4 %all-reduce = f32[4096]{0:T(1024)S(1)} all-reduce(f32[4096]{0:T(1024)S(1)} %add.74), channel_id=3, replica_groups=mesh['parts'=2,'slab'=8,'freq'=2] {'freq'}, use_global_device_ids=true, to_apply=%region_3.0.clone | all-reduce | flops 4096 | bytes 32768
  236.4 0.6 dynamic-slice.1
  (7 shorter events, 0.0 us)
Async XLA Ops:
  7.2 120.9 %reduce-scatter.2.cloned.1.call-start = ((), (), s32[]{:S(2)}) async-start(), calls=%async_computation.1 | async-start | bytes 4718592 | tf_op jit(solution)/shard_map/reduce_scatter | solution.py:35
  29.8 1.6 copy-start.6
  29.8 1.7 copy-start.5
  36.8 91.2 %copy-start.4 = (f32[2,2,2,128,128]{4,3,2,1,0:T(8,128)S(1)}, f32[2,2,2,128,128]{4,3,2,1,0:T(8,128)}, u32[]{:S(2)}) copy-start(f32[2,2,2,128,128]{4,3,2,1,0:T(8,128)} %param.9) | copy-start | bytes 1572868
  36.8 160.8 %all-gather.2.cloned.1.call-start = ((), (), s32[]{:S(2)}) async-start(), calls=%async_computation.2 | async-start | bytes 2359296 | tf_op jit(solution)/shard_map/all_gather | solution.py:37
  177.4 9.7 %copy-start.7 = (u32[32]{0:T(128)S(1)}, u32[32]{0:T(128)}, u32[]{:S(2)}) copy-start(u32[32]{0:T(128)} %constant.9) | copy-start | bytes 388
  202.0 10.5 %copy-start = (bf16[1,4096,2,256]{3,2,1,0:T(2,128)(2,1)S(1)}, bf16[1,4096,2,256]{3,2,1,0:T(2,128)(2,1)}, u32[]{:S(2)}) copy-start(bf16[1,4096,2,256]{3,2,1,0:T(2,128)(2,1)} %get-tuple-element.13) | copy-start | bytes 12582916
  212.5 8.1 %copy-start.1 = (bf16[1,4096,1,256]{1,3,2,0:T(8,128)(2,1)S(1)}, bf16[1,4096,1,256]{1,3,2,0:T(8,128)(2,1)}, u32[]{:S(2)}) copy-start(bf16[1,4096,1,256]{1,3,2,0:T(8,128)(2,1)} %copy.59) | copy-start | bytes 6291460
  212.5 8.1 %copy-start.2 = (bf16[1,4096,1,256]{1,3,2,0:T(8,128)(2,1)S(1)}, bf16[1,4096,1,256]{1,3,2,0:T(8,128)(2,1)}, u32[]{:S(2)}) copy-start(bf16[1,4096,1,256]{1,3,2,0:T(8,128)(2,1)} %copy.58) | copy-start | bytes 6291460
  212.5 8.1 %copy-start.3 = (bf16[1,4096,1,256]{1,3,2,0:T(8,128)(2,1)S(1)}, bf16[1,4096,1,256]{1,3,2,0:T(8,128)(2,1)}, u32[]{:S(2)}) copy-start(bf16[1,4096,1,256]{1,3,2,0:T(8,128)(2,1)} %copy.54) | copy-start | bytes 6291460
Sparse Core Ops, SparseCore 0:
  37.0 91.0 reduce-scatter.1
  130.2 48.7 all-gather.1
where the time goes:
time: 245 us; the launch traced here: 244 us
  waiting for transfers between devices  91 us (37%)
  local copies, waits for them, and re-layouts  73.3 us (30%)
  matrix products  32.9 us (13%)
  other arithmetic  28.2 us (12%)
  between operations  14.9 us (6%)
  blocking collectives  3.36 us (1%)
    reduce_scatter x1, waiting for transfers between devices, on_device(): own_pred = lax.psum_scatter(spread, 'slab', scatter_dimension=1, tiled=True)  91 us
    unnamed x23, local copies, waits for them, and re-layouts  39.9 us
    slice x1, local copies, waits for them, and re-layouts, on_device(): receiver_green[freq_step, :, 0] * adj_real  19.4 us
    dot_general x2, matrix products, on_device(): jnp.einsum('onu,uth->onth', source_green[freq_step], local_res[freq_step]...  18.6 us
    convert_element_type x1, other arithmetic, on_device(): (source_green * reflectivity[None, :, None, None]).astype(jnp.bfloat16)  13.2 us
    reduce_sum x1, other arithmetic, on_device(): gradient = gradient + jnp.sum(terms, axis=1)  12.4 us
    dot_general x1, matrix products, on_device(): jnp.einsum('fmas,fmbr->fasbr', scaled, receiver_green, preferred_element_...  9.45 us
    slice x1, local copies, waits for them, and re-layouts, on_device(): source_green[freq_step]  8.45 us
  transfers between devices with their start and end apart: 2, of which 1 were waited for; matrix products, arithmetic and copies ran while one was open for 28% of the time, Pallas kernels for 0%

commit v1 on v0

v1 whole, which is shorter than its diff:
```python
import functools

import jax
import jax.numpy as jnp
from jax import lax
from jax.experimental import pallas as pl
from jax.experimental.pallas import tpu as pltpu
from jax.sharding import PartitionSpec as P

RB = 4
TILE = 1024
MESH = pl.DeviceIdType.MESH
F32 = jnp.float32
BF16 = jnp.bfloat16


def forward_kernel(refl_ref, g_ref, r_ref, gd_ref, rd_ref, part_ref, g32, r32, scaled, acc):
    step = pl.program_id(1)
    lanes = g_ref.shape[2]
    points = gd_ref.shape[1]
    half = gd_ref.shape[2] // 2
    blocks = half // lanes
    rows_each = 2 * blocks
    g32[...] = g_ref[0].astype(F32)
    r32[...] = r_ref[0].astype(F32)
    weight = jnp.concatenate(
        [
            jnp.broadcast_to(refl_ref[b : b + 1, :], (lanes, lanes)).T
            for b in range(points // lanes)
        ],
        axis=0,
    )
    for block in range(blocks):
        for comp in range(2):
            rows = pl.ds(block * 2 + comp, points, stride=rows_each)
            cols = slice(comp * half + block * lanes, comp * half + (block + 1) * lanes)
            green = g32[rows, :]
            gd_ref[0, :, cols] = green.astype(BF16)
            scaled[:, cols] = (green * weight).astype(BF16)
            rd_ref[0, :, cols] = r32[rows, :].astype(BF16)
    prod = lax.dot_general(
        scaled[...], rd_ref[0], (((0,), (0,)), ((), ())), preferred_element_type=F32
    )

    @pl.when(step == 0)
    def _():
        acc[...] = prod

    @pl.when(step > 0)
    def _():
        acc[...] += prod

    @pl.when(step == pl.num_programs(1) - 1)
    def _():
        for i in range(blocks):
            for j in range(blocks):
                s_re = slice(i * lanes, (i + 1) * lanes)
                s_im = slice(half + i * lanes, half + (i + 1) * lanes)
                r_re = slice(j * lanes, (j + 1) * lanes)
                r_im = slice(half + j * lanes, half + (j + 1) * lanes)
                part_ref[0, i * blocks + j, 0] = acc[s_re, r_re] - acc[s_im, r_im]
                part_ref[0, i * blocks + j, 1] = acc[s_re, r_im] + acc[s_im, r_re]
        part_ref[0, blocks * blocks] = jnp.zeros(part_ref.shape[2:], F32)


def ring_kernel(n, snake, table_ref, part_ref, obs_ref, res_ref, adj_ref, first, held, gath,
                rs_send, rs_recv, ag_send, ag_recv):
    per = obs_ref.shape[1]
    lanes = obs_ref.shape[3]
    pairs = part_ref.shape[1] - 1
    total = n * per
    me = lax.axis_index("slab")

    def index_of(pos):
        if not snake:
            return pos
        return 2 * pos + (pos // (n // 2)) * (2 * n - 1 - 4 * pos)

    if snake:
        place = me // 2 + (me % 2) * (n - 1 - 2 * (me // 2))
    else:
        place = me
    ways = (1, -1)
    targets = tuple(index_of((place + way + n) % n) for way in ways)

    barrier = pltpu.get_barrier_semaphore()
    for target in targets:
        pl.semaphore_signal(barrier, inc=1, device_id={"slab": target}, device_id_type=MESH)
    pl.semaphore_wait(barrier, 2)

    streams = [(f, c) for c in range(2) for f in range(2)]

    def own(f, c, hop):
        owner = index_of((place - ways[f] * hop + 2 * n) % n)
        return [part_ref[f, table_ref[owner * per + k], c] for k in range(per)]

    def rs_copy(f, c, src, step):
        return pltpu.make_async_remote_copy(
            src_ref=src,
            dst_ref=held.at[f, c, step],
            send_sem=rs_send.at[f, c, step],
            recv_sem=rs_recv.at[f, c, step],
            device_id={"slab": targets[f]},
            device_id_type=MESH,
        )

    def ag_copy(f, c, step):
        owner = index_of((place - ways[f] * step + 2 * n) % n)
        view = gath.at[f, c, pl.ds(owner * per, per)]
        return pltpu.make_async_remote_copy(
            src_ref=view,
            dst_ref=view,
            send_sem=ag_send.at[f, c, step],
            recv_sem=ag_recv.at[f, c, step],
            device_id={"slab": targets[f]},
            device_id_type=MESH,
        )

    def ag_wait(f, c, step):
        owner = index_of((place - ways[f] * (step + 1) + 2 * n) % n)
        view = gath.at[f, c, pl.ds(owner * per, per)]
        pltpu.make_async_remote_copy(
            src_ref=view,
            dst_ref=view,
            send_sem=ag_send.at[f, c, step],
            recv_sem=ag_recv.at[f, c, step],
            device_id={"slab": targets[f]},
            device_id_type=MESH,
        ).wait_recv()

    for f, c in streams:
        mine = own(f, c, 1)
        for k in range(per):
            first[f, c, k] = mine[k]
        rs_copy(f, c, first.at[f, c], 0).start()

    def rs_step(step, carry):
        for f, c in streams:
            rs_copy(f, c, held.at[f, c, step], step).wait_recv()
            mine = own(f, c, step + 2)
            for k in range(per):
                held[f, c, step, k] = held[f, c, step, k] + mine[k]
            rs_copy(f, c, held.at[f, c, step], step + 1).start()
        return carry

    lax.fori_loop(0, n - 2, rs_step, 0)
    for f, c in streams:
        rs_copy(f, c, held.at[f, c, n - 2], n - 2).wait_recv()
        mine = own(f, c, n)
        for k in range(per):
            value = held[f, c, n - 2, k] + mine[k] - obs_ref[f, k, c]
            res_ref[f, k, c] = value
            gath[f, c, me * per + k] = value.astype(BF16)
        ag_copy(f, c, 0).start()

    def ag_step(step, carry):
        for f, c in streams:
            ag_wait(f, c, step)
            ag_copy(f, c, step + 1).start()
        return carry

    lax.fori_loop(0, n - 2, ag_step, 0)
    for f, c in streams:
        ag_wait(f, c, n - 2)

    def drain(step, carry):
        for f, c in streams:
            rs_copy(f, c, first.at[f, c], step).wait_send()
            ag_copy(f, c, step).wait_send()
        return carry

    lax.fori_loop(0, n - 1, drain, 0)

    side = 2
    half = side * lanes
    for f in range(2):
        for k in range(pairs):
            i, j = k // side, k % side
            panel = table_ref[total + k]
            real = gath[f, 0, panel]
            imag = gath[f, 1, panel]
            s_re = slice(i * lanes, (i + 1) * lanes)
            s_im = slice(half + i * lanes, half + (i + 1) * lanes)
            r_re = slice(j * lanes, (j + 1) * lanes)
            r_im = slice(half + j * lanes, half + (j + 1) * lanes)
            adj_ref[f, s_re, r_re] = real
            adj_ref[f, s_im, r_re] = imag
            adj_ref[f, s_re, r_im] = imag
            adj_ref[f, s_im, r_im] = -real


def adjoint_kernel(gd_ref, rd_ref, adj_ref, out_ref, total):
    step = pl.program_id(1)
    lanes = out_ref.shape[1]
    width = gd_ref.shape[2]
    points = gd_ref.shape[1]
    field = jnp.dot(gd_ref[0], adj_ref[step], preferred_element_type=F32)
    terms = field * rd_ref[0].astype(F32)
    summed = terms[:, :lanes]
    for at in range(lanes, width, lanes):
        summed = summed + terms[:, at : at + lanes]

    @pl.when(step == 0)
    def _():
        total[...] = summed

    @pl.when(step > 0)
    def _():
        total[...] += summed

    @pl.when(step == pl.num_programs(1) - 1)
    def _():
        for b in range(points // lanes):
            block = total[b * lanes : (b + 1) * lanes, :]
            out_ref[b : b + 1, :] = jnp.sum(block.T, axis=0, keepdims=True)


def interleaved_rows(green, lanes):
    freqs, points, comps, width = green.shape
    view = green.reshape(freqs, points, comps, width // lanes, lanes)
    return view.transpose(0, 1, 3, 2, 4).reshape(freqs, points * comps * width // lanes, lanes)


def on_device(reflectivity, source_green, receiver_green, observed, source_table, receiver_table):
    freqs, points, comps, width = source_green.shape
    per = observed.shape[1]
    lanes = observed.shape[3]
    n = lax.axis_size("slab")
    side = width // lanes
    pairs = side * side
    wide = comps * width
    rows_each = wide // lanes
    tiles = points // TILE
    panel_ids = (source_table[0][:, None] * RB + receiver_table[0][None, :]).reshape(-1)
    slots = jnp.arange(n * per, dtype=jnp.int32)
    hit = slots[:, None] == panel_ids[None, :]
    where_held = jnp.min(
        jnp.where(hit, jnp.arange(pairs, dtype=jnp.int32)[None, :], pairs), axis=1
    )
    table = jnp.concatenate([where_held, panel_ids]).astype(jnp.int32)

    gd, rd, part = pl.pallas_call(
        forward_kernel,
        grid=(freqs, tiles),
        in_specs=[
            pl.BlockSpec((TILE // lanes, lanes), lambda f, t: (t, 0)),
            pl.BlockSpec((1, TILE * rows_each, lanes), lambda f, t: (f, t, 0)),
            pl.BlockSpec((1, TILE * rows_each, lanes), lambda f, t: (f, t, 0)),
        ],
        out_specs=[
            pl.BlockSpec((1, TILE, wide), lambda f, t: (f, t, 0)),
            pl.BlockSpec((1, TILE, wide), lambda f, t: (f, t, 0)),
            pl.BlockSpec((1, pairs + 1, 2, lanes, lanes), lambda f, t: (f, 0, 0, 0, 0)),
        ],
        out_shape=[
            jax.ShapeDtypeStruct((freqs, points, wide), BF16),
            jax.ShapeDtypeStruct((freqs, points, wide), BF16),
            jax.ShapeDtypeStruct((freqs, pairs + 1, 2, lanes, lanes), F32),
        ],
        scratch_shapes=[
            pltpu.VMEM((TILE * rows_each, lanes), F32),
            pltpu.VMEM((TILE * rows_each, lanes), F32),
            pltpu.VMEM((TILE, wide), BF16),
            pltpu.VMEM((wide, wide), F32),
        ],
        name="forward",
    )(
        reflectivity.reshape(points // lanes, lanes),
        interleaved_rows(source_green, lanes),
        interleaved_rows(receiver_green, lanes),
    )

    vmem = pl.BlockSpec(memory_space=pltpu.VMEM)
    residual, adj = pl.pallas_call(
        functools.partial(ring_kernel, n, n == 8),
        in_specs=[pl.BlockSpec(memory_space=pltpu.SMEM), vmem, vmem],
        out_specs=[vmem, vmem],
        out_shape=[
            jax.ShapeDtypeStruct(observed.shape, F32),
            jax.ShapeDtypeStruct((freqs, wide, wide), BF16),
        ],
        scratch_shapes=[
            pltpu.VMEM((freqs, 2, per, lanes, lanes), F32),
            pltpu.VMEM((freqs, 2, n - 1, per, lanes, lanes), F32),
            pltpu.VMEM((freqs, 2, n * per, lanes, lanes), BF16),
            pltpu.SemaphoreType.DMA((freqs, 2, n - 1)),
            pltpu.SemaphoreType.DMA((freqs, 2, n - 1)),
            pltpu.SemaphoreType.DMA((freqs, 2, n - 1)),
            pltpu.SemaphoreType.DMA((freqs, 2, n - 1)),
        ],
        compiler_params=pltpu.CompilerParams(collective_id=0, has_side_effects=True),
        name="ring",
    )(table, part, observed)

    gradient = pl.pallas_call(
        adjoint_kernel,
        grid=(tiles, freqs),
        in_specs=[
            pl.BlockSpec((1, TILE, wide), lambda t, f: (f, t, 0)),
            pl.BlockSpec((1, TILE, wide), lambda t, f: (f, t, 0)),
            pl.BlockSpec((freqs, wide, wide), lambda t, f: (0, 0, 0)),
        ],
        out_specs=pl.BlockSpec((TILE // lanes, lanes), lambda t, f: (t, 0)),
        out_shape=jax.ShapeDtypeStruct((points // lanes, lanes), F32),
        scratch_shapes=[pltpu.VMEM((TILE, lanes), F32)],
        name="adjoint",
    )(gd, rd, adj)
    gradient = gradient.reshape(points)
    return (lax.psum_scatter(gradient, "freq", scatter_dimension=0, tiled=True), residual)


def solution(mesh):
    return jax.shard_map(
        on_device,
        mesh=mesh,
        in_specs=(
            P(("parts", "slab")),
            P("freq", ("parts", "slab"), None, None),
            P("freq", ("parts", "slab"), None, None),
            P("freq", ("parts", "slab"), None, None, None),
            P(("parts", "slab"), None),
            P(("parts", "slab"), None),
        ),
        out_specs=(P(("parts", "slab", "freq")), P("freq", ("parts", "slab"), None, None, None)),
        check_vma=False,
    )
```

time: 245 us -> 114 us (0.47)
  Pallas kernels: 0 us -> 105 us
  waiting for transfers between devices: 91 us -> 0 us
  local copies, waits for them, and re-layouts: 73.3 us -> 2.09 us
  matrix products: 32.9 us -> 0 us
  other arithmetic: 28.2 us -> 0.75 us
  between operations: 14.9 us -> 1.34 us
    pallas_call x0 -> x3, Pallas kernels: none -> 105 us  [the longest x1 75.2 us: on_device(): pl.pallas_call(functools.partial(ring_kernel, n, n == 8), in_specs=[pl.Bl...]
    reduce_scatter x1 -> x0, waiting for transfers between devices: 91 us -> none  [on_device(): own_pred = lax.psum_scatter(spread, 'slab', scatter_dimension=1, tiled=True)]
    unnamed x23 -> x11, local copies, waits for them, and re-layouts: 39.9 us -> 2 us
    dot_general x5 -> x0, matrix products: 32.9 us -> none  [the longest x2 18.6 us: on_device(): jnp.einsum('onu,uth->onth', source_green[freq_step], local_res[freq_step]...]
    slice x5 -> x0, local copies, waits for them, and re-layouts: 28.9 us -> none  [the longest x1 19.4 us: on_device(): receiver_green[freq_step, :, 0] * adj_real]
    convert_element_type x2 -> x0, other arithmetic: 15 us -> none  [the longest x1 13.2 us: on_device(): (source_green * reflectivity[None, :, None, None]).astype(jnp.bfloat16)]
    reduce_sum x1 -> x0, other arithmetic: 12.4 us -> none  [on_device(): gradient = gradient + jnp.sum(terms, axis=1)]
    transpose x2 -> x0, local copies, waits for them, and re-layouts: 3.58 us -> none  [the longest x1 3.22 us: on_device(): jnp.einsum('kp,fkcxy->fpcxy', onehot, partial_value, precision=lax.Precis...]
  transfers between devices with their start and end apart: 2 -> 0, of which waited for: 1 -> 0; matrix products, arithmetic and copies ran while one was open for 28% -> 0% of each run, Pallas kernels for 0% -> 0%
where the time goes in v1:
time: 114 us; the launch traced here: 113 us
  Pallas kernels  105 us (92%)
  blocking collectives  3.99 us (4%)
  local copies, waits for them, and re-layouts  2.09 us (2%)
  between operations  1.34 us (1%)
    pallas_call x1, Pallas kernels, on_device(): pl.pallas_call(functools.partial(ring_kernel, n, n == 8), in_specs=[pl.Bl...  75.2 us
    pallas_call x1, Pallas kernels, on_device(): pl.pallas_call(forward_kernel, grid=(freqs, tiles), in_specs=[pl.BlockSpe...  18 us
    pallas_call x1, Pallas kernels, on_device(): pl.pallas_call(adjoint_kernel, grid=(tiles, freqs), in_specs=[pl.BlockSpe...  12.1 us
    unnamed x1, blocking collectives  3.99 us

profile of v1, /device:TPU:0, one launch (start us, length us, event | category | flops | bytes accessed | tf_op | source)
XLA Modules:
  0.0 113.5 jit_solution(11340839263188960776)
XLA Ops:
  0.6 0.0 copy-start.2
  0.6 0.0 copy-start.1
  0.7 18.0 %forward.1 = (bf16[2,4096,512]{2,1,0:T(8,128)(2,1)}, bf16[2,4096,512]{2,1,0:T(8,128)(2,1)}, f32[2,5,2,128,128]{4,3,2,1,0:T(8,128)}) custom-call(f32[32,128]{1,0:T(8,128)} %bitcast.19, bf16[2,16384,128]{2,1,0:T(8,128)(2,1)} %bitcast.16, bf16[2,16384,128]{2,1,0:T(8,128)(2,1)} %bitcast.17), custom_call_target="tpu_custom_call" | custom-call | tf_op jit(solution)/shard_map/forward/pallas_call | solution.py:242
  18.6 0.0 copy-done.2
  18.6 0.0 copy-done.1
  18.6 0.1 broadcast_add_fusion
  18.7 0.1 add.29
  18.8 0.1 select_reduce_fusion
  18.9 0.6 pad_add_fusion.table_ref
  19.5 75.2 %ring.1 = (f32[2,2,2,128,128]{4,3,2,1,0:T(8,128)}, bf16[2,512,512]{2,1,0:T(8,128)(2,1)}) custom-call(s32[20]{0:T(128)} %pad_add_fusion.table_ref, f32[2,5,2,128,128]{4,3,2,1,0:T(8,128)} %get-tuple-element.9.part_ref, f32[2,2,2,128,128]{4,3,2,1,0:T(8,128)} %obs_ref.1), custom_call_target="tpu_custom_call" | custom-call | tf_op jit(solution)/shard_map/ring/pallas_call | solution.py:274
  94.7 0.0 copy-start.3
  94.7 0.0 copy-start
  94.7 12.1 %adjoint.1 = f32[32,128]{1,0:T(8,128)} custom-call(bf16[2,4096,512]{2,1,0:T(8,128)(2,1)} %get-tuple-element.7.gd_ref, bf16[2,4096,512]{2,1,0:T(8,128)(2,1)} %get-tuple-element.8.rd_ref, bf16[2,512,512]{2,1,0:T(8,128)(2,1)} %get-tuple-element.10.adj_ref), custom_call_target="tpu_custom_call" | custom-call | tf_op jit(solution)/shard_map/adjoint/pallas_call | solution.py:295
  106.8 4.0 %all-reduce = f32[4096]{0:T(1024)S(1)} all-reduce(f32[4096]{0:T(1024)} %bitcast.18), channel_id=2, replica_groups=mesh['parts'=2,'slab'=8,'freq'=2] {'freq'}, use_global_device_ids=true, to_apply=%region_1.2.clone | all-reduce | flops 4096 | bytes 32768
  110.8 0.0 copy-done.3
  110.8 0.6 dynamic-slice
  112.1 0.6 dynamic-slice.1
  112.7 0.0 copy-done
  112.7 0.8 copy.15
  (1 shorter events, 0.0 us)
Async XLA Ops:
  0.6 18.0 %copy-start.2 = (s32[1,2]{1,0:T(1,128)S(1)}, s32[1,2]{1,0:T(1,128)}, u32[]{:S(2)}) copy-start(s32[1,2]{1,0:T(1,128)} %param.10) | copy-start | bytes 28
  0.6 18.0 %copy-start.1 = (s32[1,2]{1,0:T(1,128)S(1)}, s32[1,2]{1,0:T(1,128)}, u32[]{:S(2)}) copy-start(s32[1,2]{1,0:T(1,128)} %param.11) | copy-start | bytes 28
  94.7 16.1 %copy-start.3 = (u32[32]{0:T(128)S(1)}, u32[32]{0:T(128)}, u32[]{:S(2)}) copy-start(u32[32]{0:T(128)} %constant.10) | copy-start | bytes 388
  94.7 18.0 %copy-start = (f32[2,2,2,128,128]{4,3,2,1,0:T(8,128)S(1)}, f32[2,2,2,128,128]{4,3,2,1,0:T(8,128)}, u32[]{:S(2)}) copy-start(f32[2,2,2,128,128]{4,3,2,1,0:T(8,128)} %get-tuple-element.15) | copy-start | bytes 1572868

commit v2 on v1

--- a/solution.py
+++ b/solution.py
@@ -82,94 +82,111 @@
         place = me
     ways = (1, -1)
     targets = tuple(index_of((place + way + n) % n) for way in ways)
+    low = (n - 1) // 2
+    high = n - 1 - low
 
     barrier = pltpu.get_barrier_semaphore()
     for target in targets:
         pl.semaphore_signal(barrier, inc=1, device_id={"slab": target}, device_id_type=MESH)
     pl.semaphore_wait(barrier, 2)
 
-    streams = [(f, c) for c in range(2) for f in range(2)]
-
-    def own(f, c, hop):
-        owner = index_of((place - ways[f] * hop + 2 * n) % n)
+    streams = [(f, c, w) for c in range(2) for f in range(2) for w in range(2)]
+    longer = [(f, c, w) for f, c, w in streams if f == w]
+
+    def hops(f, w):
+        return high if f == w else low
+
+    def own(f, c, w, away):
+        owner = index_of((place + ways[w] * away + n) % n)
         return [part_ref[f, table_ref[owner * per + k], c] for k in range(per)]
 
-    def rs_copy(f, c, src, step):
+    def rs_copy(f, c, w, src, step):
         return pltpu.make_async_remote_copy(
             src_ref=src,
-            dst_ref=held.at[f, c, step],
-            send_sem=rs_send.at[f, c, step],
-            recv_sem=rs_recv.at[f, c, step],
-            device_id={"slab": targets[f]},
+            dst_ref=held.at[f, c, w, step],
+            send_sem=rs_send.at[f, c, w, step],
+            recv_sem=rs_recv.at[f, c, w, step],
+            device_id={"slab": targets[w]},
             device_id_type=MESH,
         )
 
-    def ag_copy(f, c, step):
-        owner = index_of((place - ways[f] * step + 2 * n) % n)
+    def ag_copy(f, c, w, step, away):
+        owner = index_of((place - ways[w] * away + n) % n)
         view = gath.at[f, c, pl.ds(owner * per, per)]
         return pltpu.make_async_remote_copy(
             src_ref=view,
             dst_ref=view,
-            send_sem=ag_send.at[f, c, step],
-            recv_sem=ag_recv.at[f, c, step],
-            device_id={"slab": targets[f]},
+            send_sem=ag_send.at[f, c, w, step],
+            recv_sem=ag_recv.at[f, c, w, step],
+            device_id={"slab": targets[w]},
             device_id_type=MESH,
         )
 
-    def ag_wait(f, c, step):
-        owner = index_of((place - ways[f] * (step + 1) + 2 * n) % n)
-        view = gath.at[f, c, pl.ds(owner * per, per)]
-        pltpu.make_async_remote_copy(
-            src_ref=view,
-            dst_ref=view,
-            send_sem=ag_send.at[f, c, step],
-            recv_sem=ag_recv.at[f, c, step],
-            device_id={"slab": targets[f]},
-            device_id_type=MESH,
-        ).wait_recv()
-
-    for f, c in streams:
-        mine = own(f, c, 1)
+    def rs_pass(f, c, w, step):
+        rs_copy(f, c, w, held.at[f, c, w, step], step).wait_recv()
+        mine = own(f, c, w, hops(f, w) - step - 1)
         for k in range(per):
-            first[f, c, k] = mine[k]
-        rs_copy(f, c, first.at[f, c], 0).start()
+            held[f, c, w, step, k] = held[f, c, w, step, k] + mine[k]
+        rs_copy(f, c, w, held.at[f, c, w, step], step + 1).start()
+
+    def ag_pass(f, c, w, step):
+        ag_copy(f, c, w, step, step + 1).wait_recv()
+        ag_copy(f, c, w, step + 1, step + 1).start()
 
     def rs_step(step, carry):
-        for f, c in streams:
-            rs_copy(f, c, held.at[f, c, step], step).wait_recv()
-            mine = own(f, c, step + 2)
+        for f, c, w in streams:
+            rs_pass(f, c, w, step)
+        return carry
+
+    def ag_step(step, carry):
+        for f, c, w in streams:
+            ag_pass(f, c, w, step)
+        return carry
+
+    for f, c, w in streams:
+        mine = own(f, c, w, hops(f, w))
+        for k in range(per):
+            first[f, c, w, k] = mine[k]
+        rs_copy(f, c, w, first.at[f, c, w], 0).start()
+
+    lax.fori_loop(0, low - 1, rs_step, 0)
+    if high > low:
+        for f, c, w in longer:
+            rs_pass(f, c, w, high - 2)
+    for c in range(2):
+        for f in range(2):
+            for w in range(2):
+                last = hops(f, w) - 1
+                rs_copy(f, c, w, held.at[f, c, w, last], last).wait_recv()
+            mine = own(f, c, 0, 0)
             for k in range(per):
-                held[f, c, step, k] = held[f, c, step, k] + mine[k]
-            rs_copy(f, c, held.at[f, c, step], step + 1).start()
+                value = (
+                    held[f, c, 0, hops(f, 0) - 1, k] + held[f, c, 1, hops(f, 1) - 1, k] + mine[k]
+                ) - obs_ref[f, k, c]
+                res_ref[f, k, c] = value
+                gath[f, c, me * per + k] = value.astype(BF16)
+            for w in range(2):
+                ag_copy(f, c, w, 0, 0).start()
+
+    lax.fori_loop(0, low - 1, ag_step, 0)
+    if high > low:
+        for f, c, w in longer:
+            ag_pass(f, c, w, high - 2)
+    for f, c, w in streams:
+        last = hops(f, w) - 1
+        ag_copy(f, c, w, last, last + 1).wait_recv()
+
+    def drain(step, carry):
+        for f, c, w in streams:
+            rs_copy(f, c, w, first.at[f, c, w], step).wait_send()
+            ag_copy(f, c, w, step, step).wait_send()
         return carry
 
-    lax.fori_loop(0, n - 2, rs_step, 0)
-    for f, c in streams:
-        rs_copy(f, c, held.at[f, c, n - 2], n - 2).wait_recv()
-        mine = own(f, c, n)
-        for k in range(per):
-            value = held[f, c, n - 2, k] + mine[k] - obs_ref[f, k, c]
-            res_ref[f, k, c] = value
-            gath[f, c, me * per + k] = value.astype(BF16)
-        ag_copy(f, c, 0).start()
-
-    def ag_step(step, carry):
-        for f, c in streams:
-            ag_wait(f, c, step)
-            ag_copy(f, c, step + 1).start()
-        return carry
-
-    lax.fori_loop(0, n - 2, ag_step, 0)
-    for f, c in streams:
-        ag_wait(f, c, n - 2)
-
-    def drain(step, carry):
-        for f, c in streams:
-            rs_copy(f, c, first.at[f, c], step).wait_send()
-            ag_copy(f, c, step).wait_send()
-        return carry
-
-    lax.fori_loop(0, n - 1, drain, 0)
+    lax.fori_loop(0, low, drain, 0)
+    if high > low:
+        for f, c, w in longer:
+            rs_copy(f, c, w, first.at[f, c, w], high - 1).wait_send()
+            ag_copy(f, c, w, high - 1, high - 1).wait_send()
 
     side = 2
     half = side * lanes
@@ -280,13 +297,13 @@
             jax.ShapeDtypeStruct((freqs, wide, wide), BF16),
         ],
         scratch_shapes=[
-            pltpu.VMEM((freqs, 2, per, lanes, lanes), F32),
-            pltpu.VMEM((freqs, 2, n - 1, per, lanes, lanes), F32),
+            pltpu.VMEM((freqs, 2, 2, per, lanes, lanes), F32),
+            pltpu.VMEM((freqs, 2, 2, n // 2, per, lanes, lanes), F32),
             pltpu.VMEM((freqs, 2, n * per, lanes, lanes), BF16),
-            pltpu.SemaphoreType.DMA((freqs, 2, n - 1)),
-            pltpu.SemaphoreType.DMA((freqs, 2, n - 1)),
-            pltpu.SemaphoreType.DMA((freqs, 2, n - 1)),
-            pltpu.SemaphoreType.DMA((freqs, 2, n - 1)),
+            pltpu.SemaphoreType.DMA((freqs, 2, 2, n // 2)),
+            pltpu.SemaphoreType.DMA((freqs, 2, 2, n // 2)),
+            pltpu.SemaphoreType.DMA((freqs, 2, 2, n // 2)),
+            pltpu.SemaphoreType.DMA((freqs, 2, 2, n // 2)),
         ],
         compiler_params=pltpu.CompilerParams(collective_id=0, has_side_effects=True),
         name="ring",

time: 114 us -> 108 us (0.947)
  Pallas kernels: 105 us -> 99.7 us
    pallas_call x1, Pallas kernels: 75.2 us -> 69.6 us  [on_device(): pl.pallas_call(functools.partial(ring_kernel, n, n == 8), in_specs=[pl.Bl...]
where the time goes in v2:
time: 108 us
  Pallas kernels  99.7 us (92%)
  blocking collectives  3.99 us (4%)
  local copies, waits for them, and re-layouts  2.09 us (2%)
  between operations  1.34 us (1%)
    pallas_call x1, Pallas kernels, on_device(): pl.pallas_call(functools.partial(ring_kernel, n, n == 8), in_specs=[pl.Bl...  69.6 us
    pallas_call x1, Pallas kernels, on_device(): pl.pallas_call(forward_kernel, grid=(freqs, tiles), in_specs=[pl.BlockSpe...  18 us
    pallas_call x1, Pallas kernels, on_device(): pl.pallas_call(adjoint_kernel, grid=(tiles, freqs), in_specs=[pl.BlockSpe...  12.1 us
    unnamed x1, blocking collectives  3.99 us

profile of v2, /device:TPU:0, one launch (start us, length us, event | category | flops | bytes accessed | tf_op | source)
XLA Modules:
  0.0 107.9 jit_solution(5487049429457831858)
XLA Ops:
  0.6 0.0 copy-start.2
  0.6 0.0 copy-start.1
  0.7 18.0 %forward.1 = (bf16[2,4096,512]{2,1,0:T(8,128)(2,1)}, bf16[2,4096,512]{2,1,0:T(8,128)(2,1)}, f32[2,5,2,128,128]{4,3,2,1,0:T(8,128)}) custom-call(f32[32,128]{1,0:T(8,128)} %bitcast.19, bf16[2,16384,128]{2,1,0:T(8,128)(2,1)} %bitcast.16, bf16[2,16384,128]{2,1,0:T(8,128)(2,1)} %bitcast.17), custom_call_target="tpu_custom_call" | custom-call | tf_op jit(solution)/shard_map/forward/pallas_call | solution.py:259
  18.6 0.0 copy-done.2
  18.6 0.0 copy-done.1
  18.6 0.1 broadcast_add_fusion
  18.7 0.1 add.29
  18.8 0.1 select_reduce_fusion
  18.9 0.6 pad_add_fusion.table_ref
  19.5 69.6 %ring.1 = (f32[2,2,2,128,128]{4,3,2,1,0:T(8,128)}, bf16[2,512,512]{2,1,0:T(8,128)(2,1)}) custom-call(s32[20]{0:T(128)} %pad_add_fusion.table_ref, f32[2,5,2,128,128]{4,3,2,1,0:T(8,128)} %get-tuple-element.9.part_ref, f32[2,2,2,128,128]{4,3,2,1,0:T(8,128)} %obs_ref.1), custom_call_target="tpu_custom_call" | custom-call | tf_op jit(solution)/shard_map/ring/pallas_call | solution.py:291
  89.1 0.0 copy-start.3
  89.1 0.0 copy-start
  89.1 12.1 %adjoint.1 = f32[32,128]{1,0:T(8,128)} custom-call(bf16[2,4096,512]{2,1,0:T(8,128)(2,1)} %get-tuple-element.7.gd_ref, bf16[2,4096,512]{2,1,0:T(8,128)(2,1)} %get-tuple-element.8.rd_ref, bf16[2,512,512]{2,1,0:T(8,128)(2,1)} %get-tuple-element.10.adj_ref), custom_call_target="tpu_custom_call" | custom-call | tf_op jit(solution)/shard_map/adjoint/pallas_call | solution.py:312
  101.2 4.0 %all-reduce = f32[4096]{0:T(1024)S(1)} all-reduce(f32[4096]{0:T(1024)} %bitcast.18), channel_id=2, replica_groups=mesh['parts'=2,'slab'=8,'freq'=2] {'freq'}, use_global_device_ids=true, to_apply=%region_1.2.clone | all-reduce | flops 4096 | bytes 32768
  105.2 0.0 copy-done.3
  105.2 0.6 dynamic-slice
  106.5 0.6 dynamic-slice.1
  107.1 0.0 copy-done
  107.1 0.8 copy.15
  (1 shorter events, 0.0 us)
Async XLA Ops:
  0.6 18.0 %copy-start.2 = (s32[1,2]{1,0:T(1,128)S(1)}, s32[1,2]{1,0:T(1,128)}, u32[]{:S(2)}) copy-start(s32[1,2]{1,0:T(1,128)} %param.10) | copy-start | bytes 28
  0.6 18.0 %copy-start.1 = (s32[1,2]{1,0:T(1,128)S(1)}, s32[1,2]{1,0:T(1,128)}, u32[]{:S(2)}) copy-start(s32[1,2]{1,0:T(1,128)} %param.11) | copy-start | bytes 28
  89.1 16.1 %copy-start.3 = (u32[32]{0:T(128)S(1)}, u32[32]{0:T(128)}, u32[]{:S(2)}) copy-start(u32[32]{0:T(128)} %constant.10) | copy-start | bytes 388
  89.1 18.0 %copy-start = (f32[2,2,2,128,128]{4,3,2,1,0:T(8,128)S(1)}, f32[2,2,2,128,128]{4,3,2,1,0:T(8,128)}, u32[]{:S(2)}) copy-start(f32[2,2,2,128,128]{4,3,2,1,0:T(8,128)} %get-tuple-element.15) | copy-start | bytes 1572868
